TPU v7x, 32 devices: a whole 2x2x4 slice. The times are simulated.
32 devices in a mesh: dp: 8 (over y, x, core), head: 4 (over z).
Axes of the slice: x: 2, y: 2, z: 4, core: 2. Of those that a mesh axis runs over, the one named last changes fastest.
Arguments:
- acts: bfloat16 [8, 128, 4096], P('dp', None, 'head'), may hold values from -6 to 6
- grads: bfloat16 [8, 128, 4096], P('dp', None, 'head'), may hold values from -0.5390625 to 0.5390625
- query_acts: bfloat16 [512, 4096], P('dp', 'head'), may hold values from -6 to 6
- query_grads: bfloat16 [512, 4096], P('dp', 'head'), may hold values from -0.26953125 to 0.26953125
- basis_in: bfloat16 [4096, 4096], P('dp'), may hold values from -0.09375 to 0.09375
- basis_out: bfloat16 [4096, 4096], P('dp'), may hold values from -0.09375 to 0.09375
- damping: float32 [1], replicated, may hold values from 0.1 to 1
Outputs:
- update: bfloat16 [4096, 4096], P('dp', 'head')
- corrections: float32 [4096, 4096], P('dp', 'head')
- scores: float32 [8], replicated
All inputs are finite; a program needn't handle non-finite values.
Results may differ from a plain program's by a relative error of at most 0.0056.
Values may be sent and summed in bfloat16 or wider, within the bound.
A program may use at most 128 MiB of HBM per device.

v0:
```python
import functools
import math

import jax
import jax.numpy as jnp
from jax import lax
from jax.experimental import pallas as pl
from jax.experimental.pallas import tpu as pltpu
from jax.sharding import PartitionSpec as P

MESH = pl.DeviceIdType.MESH
ANY = pl.BlockSpec(memory_space=pl.ANY)
IN_VMEM = pl.BlockSpec(memory_space=pltpu.VMEM)
IN_SMEM = pl.BlockSpec(memory_space=pltpu.SMEM)
cores = 2
most_chunks = 8


def chunks_of(rows):
    return max(1, min(most_chunks, rows // 32))


class Place:
    def __init__(self):
        self.data_size = lax.axis_size("dp")
        self.head_size = lax.axis_size("head")
        self.chips = self.data_size // cores
        self.column_count = 2 if self.chips % 2 == 0 else 1
        self.row_count = self.chips // self.column_count
        self.data = lax.axis_index("dp")
        self.head = lax.axis_index("head")
        self.core = lax.rem(self.data, cores)
        self.chip = self.data // cores
        self.row = self.chip // self.column_count
        self.column = lax.rem(self.chip, self.column_count)

    def at(self, down=0, right=0, flip=False):
        row = lax.rem(self.row + down + self.row_count, self.row_count)
        column = lax.rem(self.column + right + self.column_count, self.column_count)
        core = (cores - 1) - self.core if flip else self.core
        return (row * self.column_count + column) * cores + core

    def enter(self):
        barrier = pltpu.get_barrier_semaphore()
        for step in range(1, self.data_size):
            other = lax.rem(self.data + step, self.data_size)
            pl.semaphore_signal(
                barrier, inc=1, device_id={"dp": other, "head": self.head}, device_id_type=MESH
            )
        for step in range(1, self.head_size):
            other = lax.rem(self.head + step, self.head_size)
            pl.semaphore_signal(
                barrier, inc=1, device_id={"dp": self.data, "head": other}, device_id_type=MESH
            )
        pl.semaphore_wait(barrier, self.data_size + self.head_size - 2)


class Copies:
    def __init__(self, place, send_sems, recv_sems, local_sems=None):
        self.place, self.send_sems, self.recv_sems = place, send_sems, recv_sems
        self.local_sems, self.used, self.local_used = local_sems, 0, 0
        self.to_drain = []

    def slot(self):
        self.used += 1
        return self.used - 1

    def make(self, slot, src, dst, data=None, head=None):
        place = self.place
        return pltpu.make_async_remote_copy(
            src_ref=src,
            dst_ref=dst,
            send_sem=self.send_sems.at[slot],
            recv_sem=self.recv_sems.at[slot],
            device_id={
                "dp": place.data if data is None else data,
                "head": place.head if head is None else head,
            },
            device_id_type=MESH,
        )

    def send(self, src, dst, data=None, head=None):
        copy = self.make(self.slot(), src, dst, data, head)
        copy.start()
        self.to_drain.append(copy.wait_send)
        return copy

    def local(self, src, dst):
        copy = pltpu.make_async_copy(src, dst, self.local_sems.at[self.local_used])
        self.local_used += 1
        copy.start()
        return copy

    def drain(self):
        for wait in self.to_drain:
            wait()


class PlaneGather:
    def __init__(self, copies, own, slot, rows):
        self.copies, self.own, self.slot, self.rows = copies, own, slot, rows
        low = max(rows // 2 // 16 * 16, 1)
        self.low, self.high = (0, low), (low, rows - low)

    def first(self):
        c, place = self.copies, self.copies.place
        self.right, self.down = {}, {}
        for right_half, down_half in ((self.low, self.high), (self.high, self.low)):
            for right in range(1, place.column_count):
                self.right[right, right_half] = c.send(
                    self.own(*right_half),
                    self.slot(place.data, *right_half),
                    place.at(right=right),
                )
            for down in range(1, place.row_count):
                self.down[down, down_half] = c.send(
                    self.own(*down_half), self.slot(place.data, *down_half), place.at(down=down)
                )
        whole = (0, self.rows)
        self.flips = [
            c.send(self.own(*whole), self.slot(place.data, *whole), place.at(flip=True))
        ]

    def flip(self, index):
        place = self.copies.place
        block = self.slot(index, 0, self.rows)
        self.flips.append(self.copies.send(block, block, place.at(flip=True)))

    def second(self):
        c, place = self.copies, self.copies.place
        self.corner = {}
        for right in range(1, place.column_count):
            self.right[right, self.low].wait_recv()
            block = self.slot(place.at(right=-right), *self.low)
            for down in range(1, place.row_count):
                self.corner[down, right, 0] = c.send(block, block, place.at(down=down))
        for down in range(1, place.row_count):
            self.down[down, self.high].wait_recv()
            block = self.slot(place.at(down=-down), *self.high)
            for right in range(1, place.column_count):
                self.corner[down, right, 1] = c.send(block, block, place.at(right=right))

    def third(self):
        place = self.copies.place
        for right in range(1, place.column_count):
            self.right[right, self.high].wait_recv()
            self.flip(place.at(right=-right))
        for down in range(1, place.row_count):
            self.down[down, self.low].wait_recv()
            self.flip(place.at(down=-down))

    def fourth(self):
        place = self.copies.place
        for down in range(1, place.row_count):
            for right in range(1, place.column_count):
                self.corner[down, right, 0].wait_recv()
                self.corner[down, right, 1].wait_recv()
                self.flip(place.at(down=-down, right=-right))

    def last(self):
        for copy in self.flips:
            copy.wait_recv()


class LineGather:
    def __init__(self, copies, own, slot):
        self.copies, self.own, self.slot = copies, own, slot
        steps = range(1, copies.place.head_size)
        self.up = {step: copies.slot() for step in steps}
        self.down = {step: copies.slot() for step in steps}

    def hand_on(self, step):
        place = self.copies.place
        head, size = place.head, place.head_size
        for slots, sign in ((self.up, 1), (self.down, -1)):
            owner = head - sign * (step - 1)
            inside = (head + sign >= 0) & (head + sign < size) & (owner >= 0) & (owner < size)

            def copy(slots=slots, sign=sign, owner=owner):
                src = self.own if step == 1 else self.slot(owner)
                return self.copies.make(
                    slots[step], src, self.slot(owner), head=head + sign
                )

            pl.when(inside)(lambda copy=copy: copy().start())

            def drain(copy=copy, inside=inside):
                pl.when(inside)(lambda: copy().wait_send())

            self.copies.to_drain.append(drain)

    def arrive(self, step):
        place = self.copies.place
        head, size = place.head, place.head_size
        for slots, sign in ((self.up, 1), (self.down, -1)):
            owner = head - sign * step

            def wait(slots=slots, owner=owner):
                block = self.slot(owner)
                self.copies.make(slots[step], block, block, head=head).wait_recv()

            pl.when((owner >= 0) & (owner < size))(wait)


def gather_inputs_kernel(
    acts, grads, basis_in, basis_out, columns, acts_full, grads_wide, grads_chip, basis_pair,
    held_columns, held_acts, held_grads, send_sems, recv_sems, local_sems,
):
    place = Place()
    c = Copies(place, send_sems, recv_sems, local_sems)
    head, size = place.head, place.head_size
    width = acts.shape[1]
    rows, block = columns.shape[1], basis_pair.shape[2]
    chip_width = grads_chip.shape[2]
    span = pl.ds(pl.multiple_of(head * width, width), width)
    place.enter()
    wide = []
    for step in range(1, size):
        other = lax.rem(head + step, size)
        wide.append(c.send(grads.at[other], grads_wide.at[:, span], head=other))
    line = LineGather(
        c,
        acts,
        lambda owner: acts_full.at[:, pl.ds(pl.multiple_of(owner * width, width), width)],
    )
    line.hand_on(1)
    plane = PlaneGather(
        c,
        lambda low, count: basis_in.at[pl.ds(low, count), span],
        lambda index, low, count: columns.at[index, pl.ds(low, count), :],
        rows,
    )
    plane.first()
    pairs = []
    for chip in range(place.chips):
        start = pl.multiple_of((chip * cores + (cores - 1) - place.core) * block, block)
        pairs.append(
            c.send(basis_out.at[:, pl.ds(start, block)], basis_pair.at[chip], place.at(flip=True))
        )
    loads = [
        c.local(grads.at[head], held_grads),
        c.local(acts, held_acts),
        c.local(basis_in.at[:, span], held_columns),
    ]
    for load in loads:
        load.wait()
    stores = [
        c.local(held_grads, grads_wide.at[:, span]),
        c.local(held_acts, acts_full.at[:, span]),
        c.local(held_columns, columns.at[place.data]),
    ]
    stores[0].wait()
    for copy in wide:
        copy.wait_recv()

    def chip_span(chip):
        return pl.ds(pl.multiple_of(chip * chip_width, chip_width), chip_width)

    across, flips = [], []
    mine = c.local(grads_wide.at[:, chip_span(place.chip)], grads_chip.at[place.data])
    for step in range(1, place.chips):
        chip = lax.rem(place.chip + step, place.chips)
        across.append(
            c.send(
                grads_wide.at[:, chip_span(chip)],
                grads_chip.at[place.data],
                chip * cores + place.core,
            )
        )
    flips.append(
        c.send(
            grads_wide.at[:, chip_span(place.chip)],
            grads_chip.at[place.data],
            place.at(flip=True),
        )
    )
    for step in range(1, size - 1):
        line.arrive(step)
        line.hand_on(step + 1)
    plane.second()
    for step, copy in zip(range(1, place.chips), across):
        copy.wait_recv()
        source = lax.rem(place.chip - step + place.chips, place.chips) * cores + place.core
        flips.append(c.send(grads_chip.at[source], grads_chip.at[source], place.at(flip=True)))
    plane.third()
    plane.fourth()
    if size > 1:
        line.arrive(size - 1)
    plane.last()
    for copy in pairs + flips:
        copy.wait_recv()
    mine.wait()
    for store in stores[1:]:
        store.wait()
    c.drain()


def scatter_kernel(parts, landed, held, send_sems, recv_sems, local_sems):
    place = Place()
    c = Copies(place, send_sems, recv_sems, local_sems)
    place.enter()
    sent = []
    for step in range(1, place.chips):
        chip = lax.rem(place.chip + step, place.chips)
        sent.append(
            c.send(parts.at[chip], landed.at[place.chip], chip * cores + place.core)
        )
    c.local(parts.at[place.chip], held).wait()
    c.local(held, landed.at[place.chip]).wait()
    for copy in sent:
        copy.wait_recv()
    c.drain()


def gather_rotated_kernel(
    rotated_out, rotated_in, out_all, in_all, held_out, held_in, send_sems, recv_sems, local_sems
):
    place = Place()
    c = Copies(place, send_sems, recv_sems, local_sems)
    place.enter()
    line = LineGather(c, rotated_out, lambda owner: out_all.at[:, owner])
    line.hand_on(1)
    plane = PlaneGather(
        c,
        lambda low, count: rotated_in.at[pl.ds(low, count), :],
        lambda index, low, count: in_all.at[index, pl.ds(low, count), :],
        rotated_in.shape[0],
    )
    plane.first()
    loads = [c.local(rotated_out, held_out), c.local(rotated_in, held_in)]
    for load in loads:
        load.wait()
    stores = [c.local(held_out, out_all.at[:, place.head]), c.local(held_in, in_all.at[place.data])]
    plane.second()
    plane.third()
    for step in range(1, place.head_size):
        line.arrive(step)
        if step + 1 < place.head_size:
            line.hand_on(step + 1)
        if step == 1:
            plane.fourth()
    if place.head_size == 1:
        plane.fourth()
    plane.last()
    for store in stores:
        store.wait()
    c.drain()


def tile_kernel(
    seq_here, seq_len, damping, out_all, in_all, corrections, scaled, scores, products
):
    data_size = out_all.shape[0]
    train_rows = seq_here * seq_len
    seq_count = data_size * seq_here

    def product(left, right):
        return lax.dot_general(
            left, right, (((0,), (0,)), ((), ())), preferred_element_type=jnp.float32
        )

    total = jnp.zeros(corrections.shape, jnp.float32)
    for seq in range(seq_count):
        owner, start = seq // seq_here, (seq % seq_here) * seq_len
        rows = slice(start, start + seq_len)
        value = product(out_all[owner, rows, :], in_all[owner, rows, :])
        products[seq] = value
        total = total + value * value
    mean = total / seq_count
    corrections[...] = mean
    query_out = out_all[:, train_rows:, :].reshape(-1, out_all.shape[2])
    query_in = in_all[:, train_rows:, :].reshape(-1, in_all.shape[2])
    ratio = (product(query_out, query_in) / (mean + damping[0])).astype(jnp.bfloat16)
    scaled[...] = ratio
    weights = ratio.astype(jnp.float32)
    for seq in range(seq_count):
        scores[0, seq, :] = jnp.sum(products[seq] * weights, axis=0)


def invert_kernel(
    parts, partial_scores, back_all, scores, rising, falling, mine, score_line, score_plane,
    score_sum, send_sems, recv_sems, local_sems,
):
    place = Place()
    c = Copies(place, send_sems, recv_sems, local_sems)
    head, size = place.head, place.head_size
    rows, width = mine.shape
    chunk_count = chunks_of(rows)
    count = rows // chunk_count
    place.enter()

    line_sent = []
    for step in range(1, size):
        other = lax.rem(head + step, size)
        line_sent.append(c.send(partial_scores, score_line.at[step], head=other))
    slots = {}
    for chunk in range(chunk_count):
        for target in range(size):
            for sign in (1, -1):
                slots[chunk, target, sign] = c.slot()

    def message(chunk, target, sign, first):
        span = pl.ds(chunk * count, count)
        buffer = rising if sign == 1 else falling
        block = buffer.at[target, span, :]
        src = parts.at[span, pl.ds(target * width, width)] if first else block
        return c.make(slots[chunk, target, sign], src, block, head=head + sign)

    def arrived(chunk, target, sign):
        span = pl.ds(chunk * count, count)
        block = (rising if sign == 1 else falling).at[target, span, :]
        c.make(slots[chunk, target, sign], block, block, head=head).wait_recv()

    def own_part(chunk, target):
        return parts[
            chunk * count : (chunk + 1) * count, target * width : (target + 1) * width
        ].astype(jnp.float32)

    orders = {1: list(range(size - 1, 0, -1)), -1: list(range(size - 1))}
    def begin(chunk):
        for sign in (1, -1):
            end = 0 if sign == 1 else size - 1
            for target in orders[sign]:
                pl.when(head == end)(
                    lambda target=target, sign=sign: message(chunk, target, sign, True).start()
                )
                ahead = head < target if sign == 1 else head > target

                def drain(target=target, sign=sign, ahead=ahead):
                    pl.when(ahead)(lambda: message(chunk, target, sign, False).wait_send())

                c.to_drain.append(drain)

    def add(chunk, target, sign):
        span = slice(chunk * count, (chunk + 1) * count)
        arrived(chunk, target, sign)
        buffer = rising if sign == 1 else falling
        buffer[target, span, :] = (
            buffer[target, span, :].astype(jnp.float32) + own_part(chunk, target)
        ).astype(buffer.dtype)
        message(chunk, target, sign, False).start()

    def pass_on(chunk, distance):
        for sign in (1, -1):
            here = distance if sign == 1 else size - 1 - distance

            @pl.when(head == here)
            def passes(sign=sign, here=here):
                for target in orders[sign]:
                    if (target - here) * sign > 0:
                        add(chunk, target, sign)

    def finish_chunk(chunk):
        span = slice(chunk * count, (chunk + 1) * count)
        for target in range(size):

            @pl.when(head == target)
            def finish(target=target):
                total = own_part(chunk, target)
                if target > 0:
                    arrived(chunk, target, 1)
                    total = total + rising[target, span, :].astype(jnp.float32)
                if target < size - 1:
                    arrived(chunk, target, -1)
                    total = total + falling[target, span, :].astype(jnp.float32)
                mine[span, :] = total.astype(mine.dtype)

    planes, stores, plane_sent = [], [], []
    lag = max(size - 2, 1)
    begin(0)
    for turn in range(chunk_count + lag + 2):
        if turn + 1 < chunk_count:
            begin(turn + 1)
        for distance in range(1, size - 1):
            if 0 <= turn - distance + 1 < chunk_count:
                pass_on(turn - distance + 1, distance)
        if 0 <= turn - lag < chunk_count:
            chunk = turn - lag
            finish_chunk(chunk)
            base = chunk * count
            plane = PlaneGather(
                c,
                lambda low, n, base=base: mine.at[pl.ds(base + low, n), :],
                lambda index, low, n, base=base: back_all.at[index, pl.ds(base + low, n), :],
                count,
            )
            plane.first()
            stores.append(
                c.local(
                    mine.at[pl.ds(base, count), :],
                    back_all.at[place.data, pl.ds(base, count), :],
                )
            )
            planes.append(plane)
        if 0 <= turn - lag - 1 < chunk_count:
            planes[turn - lag - 1].second()
            planes[turn - lag - 1].third()
        if 0 <= turn - lag - 2 < chunk_count:
            planes[turn - lag - 2].fourth()
        if turn == 0:
            total = partial_scores[...]
            for step, copy in zip(range(1, size), line_sent):
                copy.wait_recv()
                total = total + score_line[step]
            score_sum[...] = total
            for step in range(1, place.data_size):
                other = lax.rem(place.data + step, place.data_size)
                plane_sent.append(c.send(score_sum, score_plane.at[step], other))
    total = score_sum[...]
    for step, copy in zip(range(1, place.data_size), plane_sent):
        copy.wait_recv()
        total = total + score_plane[step]
    scores[...] = total
    for plane in planes:
        plane.last()
    for store in stores:
        store.wait()
    c.drain()


def sems(remote, local):
    return [
        pltpu.SemaphoreType.DMA((remote,)),
        pltpu.SemaphoreType.DMA((remote,)),
        pltpu.SemaphoreType.DMA((local,)),
    ]


def talking(number):
    return pltpu.CompilerParams(collective_id=number, has_side_effects=True)


def shaped(*shape, dtype=jnp.bfloat16):
    return jax.ShapeDtypeStruct(shape, dtype)


def per_device(acts, grads, query_acts, query_grads, basis_in, basis_out, damping):
    seq_here, seq_len, width = acts.shape
    data_size = lax.axis_size("dp")
    head_size = lax.axis_size("head")
    chips = data_size // cores
    chunk_count = chunks_of(basis_out.shape[1] // data_size)
    basis_rows, full_in = basis_in.shape
    full_out = basis_out.shape[1]
    block = full_out // data_size
    grads_width = grads.shape[2]
    train_rows = seq_here * seq_len
    acts_rows = jnp.concatenate([acts.reshape(train_rows, width), query_acts], axis=0)
    grads_rows = jnp.concatenate([grads.reshape(train_rows, grads_width), query_grads], axis=0)
    row_count = acts_rows.shape[0]
    share = row_count // head_size
    chip_width = full_out // chips
    bf16 = jnp.bfloat16
    gather_copies = 8 * data_size + 4 * head_size

    columns, acts_full, ignored, grads_chip, basis_pair = pl.pallas_call(
        gather_inputs_kernel,
        out_shape=(
            shaped(data_size, basis_rows, width),
            shaped(row_count, full_in),
            shaped(share, full_out),
            shaped(data_size, share, chip_width),
            shaped(chips, basis_rows, block),
        ),
        in_specs=[ANY] * 4,
        out_specs=(ANY,) * 5,
        scratch_shapes=[
            pltpu.VMEM((basis_rows, width), bf16),
            pltpu.VMEM((row_count, width), bf16),
            pltpu.VMEM((share, grads_width), bf16),
        ]
        + sems(gather_copies, 8),
        compiler_params=talking(0),
        name="gather_inputs",
    )(acts_rows, grads_rows.reshape(head_size, share, grads_width), basis_in, basis_out)
    columns = columns.reshape(full_in, width)

    core = lax.rem(lax.axis_index("dp"), cores)
    grads_pair = grads_chip.reshape(data_size * share, chip_width)
    own_grads = lax.dynamic_slice_in_dim(grads_pair, core * basis_rows, basis_rows, 1)
    pair_grads = lax.dynamic_slice_in_dim(
        grads_pair, ((cores - 1) - core) * basis_rows, basis_rows, 1
    )
    own_parts = [
        jnp.dot(
            own_grads,
            lax.dynamic_slice_in_dim(basis_out, (chip * cores + core) * block, block, 1),
            preferred_element_type=jnp.float32,
        )
        + jnp.dot(pair_grads, basis_pair[chip], preferred_element_type=jnp.float32)
        for chip in range(chips)
    ]
    parts = jnp.stack([part.astype(bf16) for part in own_parts])
    landed = pl.pallas_call(
        scatter_kernel,
        out_shape=shaped(chips, data_size * share, block),
        in_specs=[ANY],
        out_specs=ANY,
        scratch_shapes=[pltpu.VMEM((data_size * share, block), bf16)] + sems(chips, 2),
        compiler_params=talking(1),
        name="scatter_rotated",
    )(parts)
    rotated_out = jnp.sum(landed.astype(jnp.float32), axis=0).astype(bf16)
    rotated_in = jnp.dot(acts_full, columns, preferred_element_type=jnp.float32).astype(bf16)
    out_all, in_all = pl.pallas_call(
        gather_rotated_kernel,
        out_shape=(
            shaped(data_size, head_size, share, block),
            shaped(data_size, row_count, width),
        ),
        in_specs=[ANY] * 2,
        out_specs=(ANY,) * 2,
        scratch_shapes=[
            pltpu.VMEM((data_size, share, block), bf16),
            pltpu.VMEM((row_count, width), bf16),
        ]
        + sems(gather_copies, 8),
        compiler_params=talking(2),
        name="gather_rotated",
    )(rotated_out.reshape(data_size, share, block), rotated_in)
    out_all = out_all.reshape(data_size, row_count, block)

    seq_count = data_size * seq_here
    tile = min(width, 256)
    steps = width // tile
    corrections, scaled, tile_scores = pl.pallas_call(
        functools.partial(tile_kernel, seq_here, seq_len),
        grid=(steps,),
        out_shape=(
            shaped(block, width, dtype=jnp.float32),
            shaped(block, width),
            shaped(steps, seq_count, tile, dtype=jnp.float32),
        ),
        in_specs=[
            IN_SMEM,
            pl.BlockSpec((data_size, row_count, block), lambda i: (0, 0, 0)),
            pl.BlockSpec((data_size, row_count, tile), lambda i: (0, 0, i)),
        ],
        out_specs=(
            pl.BlockSpec((block, tile), lambda i: (0, i)),
            pl.BlockSpec((block, tile), lambda i: (0, i)),
            pl.BlockSpec((1, seq_count, tile), lambda i: (i, 0, 0)),
        ),
        scratch_shapes=[pltpu.VMEM((seq_count, block, tile), jnp.float32)],
        name="fit_tile",
    )(damping, out_all, in_all)

    back_parts = lax.dot_general(
        scaled, columns, (((1,), (1,)), ((), ())), preferred_element_type=jnp.float32
    ).astype(bf16)
    partial_scores = jnp.broadcast_to(
        jnp.sum(tile_scores, axis=(0, 2))[:, None], (seq_count, 128)
    )
    back_all, score_sums = pl.pallas_call(
        invert_kernel,
        out_shape=(
            shaped(data_size, block, width),
            shaped(seq_count, 128, dtype=jnp.float32),
        ),
        in_specs=[IN_VMEM] * 2,
        out_specs=(ANY, IN_VMEM),
        scratch_shapes=[
            pltpu.VMEM((head_size, block, width), bf16),
            pltpu.VMEM((head_size, block, width), bf16),
            pltpu.VMEM((block, width), bf16),
            pltpu.VMEM((head_size, seq_count, 128), jnp.float32),
            pltpu.VMEM((data_size, seq_count, 128), jnp.float32),
            pltpu.VMEM((seq_count, 128), jnp.float32),
        ]
        + sems(
            chunk_count * (8 * data_size + 2 * head_size) + data_size + head_size, chunk_count
        ),
        compiler_params=talking(3),
        name="invert",
    )(back_parts, partial_scores)
    scores = score_sums[:, 0] / math.sqrt(full_in * full_out)
    update = jnp.dot(
        basis_out, back_all.reshape(full_out, width), preferred_element_type=jnp.float32
    ).astype(bf16)
    return (update, corrections, scores)


def solution(mesh):
    in_specs = (
        P("dp", None, "head"),
        P("dp", None, "head"),
        P("dp", "head"),
        P("dp", "head"),
        P("dp", None),
        P("dp", None),
        P(),
    )
    out_specs = (P("dp", "head"), P("dp", "head"), P())
    return jax.shard_map(
        per_device, mesh=mesh, in_specs=in_specs, out_specs=out_specs, check_vma=False
    )
```

profile of v0, /device:TPU:11, one launch (start us, length us, event | category | flops | bytes accessed | tf_op | source)
XLA Modules:
  0.0 252.0 jit_solution(85821174328575340)
XLA Ops:
  1.3 1.8 pad_maximum_fusion.1.acts
  3.1 1.8 pad_maximum_fusion.2
  4.9 48.1 %gather_inputs.1 = (bf16[8,512,1024]{2,1,0:T(8,128)(2,1)}, bf16[192,4096]{1,0:T(8,128)(2,1)}, bf16[48,4096]{1,0:T(8,128)(2,1)}, bf16[8,48,1024]{2,1,0:T(8,128)(2,1)}, bf16[4,512,512]{2,1,0:T(8,128)(2,1)}) custom-call(bf16[192,1024]{1,0:T(8,128)(2,1)} %pad_maximum_fusion.1.acts, bf16[4,48,1024]{2,1,0:T(8,128)(2,1)} %bitcast.44, bf16[512,4096]{1,0:T(8,128)(2,1)} %basis_in.1, ...), custom_call_target="tpu_custom_call" | custom-call | tf_op jit(solution)/shard_map/gather_inputs/pallas_call | solution.py:556
  53.0 0.0 copy-start
  53.0 0.0 copy-start.1
  53.0 0.0 copy-start.2
  53.0 6.6 %convolution_convert_fusion.2.rotated_in = bf16[192,1024]{1,0:T(8,128)(2,1)} fusion(bf16[192,4096]{1,0:T(8,128)(2,1)} %get-tuple-element.16, bf16[4096,1024]{1,0:T(8,128)(2,1)} %bitcast.49), kind=kOutput, calls=%fused_computation.8 | convolution fusion | flops 1610809344 | bytes 10354688 | tf_op jit(solution)/shard_map/dot_general | solution.py:604
  59.6 0.0 copy-done
  59.6 0.0 copy-done.1
  59.6 0.4 fusion.20
  60.0 0.0 copy-done.2
  60.0 0.4 fusion.7
  60.3 0.4 fusion.17
  60.7 0.4 fusion.6
  61.1 0.4 fusion.14
  61.5 0.4 fusion.5
  61.9 0.4 fusion.23
  62.2 0.4 fusion.8
  62.6 1.3 pad_maximum_fusion.parts
  64.0 20.8 %scatter_rotated.1 = bf16[4,384,512]{2,1,0:T(8,128)(2,1)} custom-call(bf16[4,384,512]{2,1,0:T(8,128)(2,1)} %pad_maximum_fusion.parts), custom_call_target="tpu_custom_call" | custom-call | tf_op jit(solution)/shard_map/scatter_rotated/pallas_call | solution.py:594
  84.8 2.5 reduce_sum.21
  87.3 29.6 %gather_rotated.1 = (bf16[8,4,48,512]{3,2,1,0:T(8,128)(2,1)}, bf16[8,192,1024]{2,1,0:T(8,128)(2,1)}) custom-call(bf16[8,48,512]{2,1,0:T(8,128)(2,1)} %bitcast.46, bf16[192,1024]{1,0:T(8,128)(2,1)} %convolution_convert_fusion.2.rotated_in), custom_call_target="tpu_custom_call" | custom-call | tf_op jit(solution)/shard_map/gather_rotated/pallas_call | solution.py:605
  116.9 7.6 %fit_tile.1 = (f32[512,1024]{1,0:T(8,128)}, bf16[512,1024]{1,0:T(8,128)(2,1)}, f32[4,8,256]{2,1,0:T(8,128)}) custom-call(f32[1]{0:T(128)S(6)} %copy.12.damping, bf16[8,192,512]{2,1,0:T(8,128)(2,1)} %bitcast.45, bf16[8,192,1024]{2,1,0:T(8,128)(2,1)} %get-tuple-element.19.in_all), custom_call_target="tpu_custom_call" | custom-call | tf_op jit(solution)/shard_map/fit_tile/pallas_call | solution.py:626
  124.5 0.0 copy-start.3
  124.5 10.2 %convolution_convert_fusion.parts = bf16[512,4096]{1,0:T(8,128)(2,1)} fusion(bf16[512,1024]{1,0:T(8,128)(2,1)} %get-tuple-element.20, bf16[4096,1024]{1,0:T(8,128)(2,1)} %bitcast.50), kind=kOutput, calls=%fused_computation | convolution fusion | flops 4297064448 | bytes 13631488 | tf_op jit(solution)/shard_map/dot_general | solution.py:648
  134.7 0.0 copy-done.3
  134.7 0.1 reduce_sum.22
  134.9 0.7 broadcast_in_dim.2.partial_scores
  135.5 105.4 %invert.1 = (bf16[8,512,1024]{2,1,0:T(8,128)(2,1)}, f32[8,128]{1,0:T(8,128)}) custom-call(bf16[512,4096]{1,0:T(8,128)(2,1)} %convolution_convert_fusion.parts, f32[8,128]{1,0:T(8,128)} %broadcast_in_dim.2.partial_scores), custom_call_target="tpu_custom_call" | custom-call | tf_op jit(solution)/shard_map/invert/pallas_call | solution.py:654
  241.0 0.0 copy-start.4
  241.0 9.1 %fusion = bf16[512,1024]{0,1:T(8,128)(2,1)S(1)} fusion(bf16[4096,1024]{1,0:T(8,128)(2,1)} %bitcast.51, bf16[512,4096]{1,0:T(8,128)(2,1)} %basis_out.1), kind=kOutput, calls=%fused_computation.3 | convolution fusion | flops 4295491584 | bytes 13631488 | tf_op jit(solution)/shard_map/dot_general | solution.py:677
  250.1 1.3 copy.11
  251.4 0.0 copy-done.4
  251.4 0.6 multiply_reduce_fusion
Async XLA Ops:
  53.0 6.6 %copy-start = (bf16[8,48,1024]{2,1,0:T(8,128)(2,1)S(1)}, bf16[8,48,1024]{2,1,0:T(8,128)(2,1)}, u32[]{:S(2)}) copy-start(bf16[8,48,1024]{2,1,0:T(8,128)(2,1)} %get-tuple-element.14) | copy-start | bytes 2359300
  53.0 6.6 %copy-start.1 = (bf16[512,4096]{1,0:T(8,128)(2,1)S(1)}, bf16[512,4096]{1,0:T(8,128)(2,1)}, u32[]{:S(2)}) copy-start(bf16[512,4096]{1,0:T(8,128)(2,1)} %basis_out.1) | copy-start | bytes 12582916
  53.0 7.0 %copy-start.2 = (bf16[4,512,512]{2,1,0:T(8,128)(2,1)S(1)}, bf16[4,512,512]{2,1,0:T(8,128)(2,1)}, u32[]{:S(2)}) copy-start(bf16[4,512,512]{2,1,0:T(8,128)(2,1)} %get-tuple-element.15) | copy-start | bytes 6291460
  124.5 10.2 %copy-start.3 = (f32[4,8,256]{2,1,0:T(8,128)S(1)}, f32[4,8,256]{2,1,0:T(8,128)}, u32[]{:S(2)}) copy-start(f32[4,8,256]{2,1,0:T(8,128)} %get-tuple-element.21) | copy-start | bytes 98308
  241.0 10.4 %copy-start.4 = (f32[8,128]{1,0:T(8,128)S(1)}, f32[8,128]{1,0:T(8,128)}, u32[]{:S(2)}) copy-start(f32[8,128]{1,0:T(8,128)} %get-tuple-element.24) | copy-start | bytes 12292
where the time goes:
time: 254 us; the launch traced here: 252 us
  Pallas kernels  212 us (83%)
  matrix products  28.9 us (11%)
  other arithmetic  8.17 us (3%)
    pallas_call x1, Pallas kernels, per_device(): pl.pallas_call(invert_kernel, out_shape=(shaped(data_size, block, width),...  105 us
    pallas_call x1, Pallas kernels, per_device(): pl.pallas_call(gather_inputs_kernel, out_shape=(shaped(data_size, basis_r...  48.1 us
    pallas_call x1, Pallas kernels, per_device(): pl.pallas_call(gather_rotated_kernel, out_shape=(shaped(data_size, head_s...  29.6 us
    pallas_call x1, Pallas kernels, per_device(): pl.pallas_call(scatter_kernel, out_shape=shaped(chips, data_size * share,...  20.8 us
    dot_general x1, matrix products, per_device(): lax.dot_general(scaled, columns, (((1,), (1,)), ((), ())), preferred_elem...  10.2 us
    dot_general x1, matrix products, per_device(): jnp.dot(basis_out, back_all.reshape(full_out, width), preferred_element_t...  9.11 us
    pallas_call x1, Pallas kernels, per_device(): pl.pallas_call(functools.partial(tile_kernel, seq_here, seq_len), grid=(s...  7.58 us
    dot_general x1, matrix products, per_device(): jnp.dot(acts_full, columns, preferred_element_type=jnp.float32).astype(bf16)  6.58 us

commit v1 on v0

--- a/solution.py
+++ b/solution.py
@@ -13,11 +13,8 @@
 IN_VMEM = pl.BlockSpec(memory_space=pltpu.VMEM)
 IN_SMEM = pl.BlockSpec(memory_space=pltpu.SMEM)
 cores = 2
-most_chunks = 8
-
-
-def chunks_of(rows):
-    return max(1, min(most_chunks, rows // 32))
+most_columns = 256
+halves = 2
 
 
 class Place:
@@ -377,144 +374,187 @@
         scores[0, seq, :] = jnp.sum(products[seq] * weights, axis=0)
 
 
-def invert_kernel(
-    parts, partial_scores, back_all, scores, rising, falling, mine, score_line, score_plane,
-    score_sum, send_sems, recv_sems, local_sems,
+def finish_kernel(
+    scaled, columns, basis, partial_scores, update, scores, held_columns, held_basis, rising,
+    falling, back, whole_part, score_line, score_plane, score_sum, line_send, line_recv,
+    plane_send, plane_recv, flip_send, flip_recv, score_send, score_recv, local_sems,
 ):
     place = Place()
-    c = Copies(place, send_sems, recv_sems, local_sems)
     head, size = place.head, place.head_size
-    rows, width = mine.shape
-    chunk_count = chunks_of(rows)
-    count = rows // chunk_count
+    rows, width = scaled.shape
+    turns, piece = rising.shape[1], rising.shape[3]
+    halves = line_send.shape[3]
+    half_rows = rows // halves
+    loads = [
+        pltpu.make_async_copy(columns, held_columns, local_sems.at[0]),
+        pltpu.make_async_copy(basis, held_basis, local_sems.at[1]),
+    ]
+    for load in loads:
+        load.start()
     place.enter()
-
+    c = Copies(place, score_send, score_recv)
     line_sent = []
     for step in range(1, size):
         other = lax.rem(head + step, size)
         line_sent.append(c.send(partial_scores, score_line.at[step], head=other))
-    slots = {}
-    for chunk in range(chunk_count):
-        for target in range(size):
+    plane_slots = {step: c.slot() for step in range(1, place.data_size)}
+
+    def plane_score(step):
+        other = lax.rem(place.data + step, place.data_size)
+        return c.make(plane_slots[step], score_sum, score_plane.at[step], other)
+
+    def span(half):
+        return pl.ds(half * half_rows, half_rows)
+
+    def product(target, turn):
+        start = pl.multiple_of(target * width + turn * piece, piece)
+        whole_part[...] = lax.dot_general(
+            scaled[...],
+            held_columns[pl.ds(start, piece), :],
+            (((1,), (1,)), ((), ())),
+            preferred_element_type=jnp.float32,
+        )
+
+    def message(sign, target, turn, half):
+        block = (rising if sign == 1 else falling).at[target, turn, span(half), :]
+        way = 0 if sign == 1 else 1
+        return pltpu.make_async_remote_copy(
+            src_ref=block,
+            dst_ref=block,
+            send_sem=line_send.at[way, target, turn, half],
+            recv_sem=line_recv.at[way, target, turn, half],
+            device_id={"dp": place.data, "head": head + sign},
+            device_id_type=MESH,
+        )
+
+    def each_target(visit):
+        def step(index, carry):
             for sign in (1, -1):
-                slots[chunk, target, sign] = c.slot()
-
-    def message(chunk, target, sign, first):
-        span = pl.ds(chunk * count, count)
-        buffer = rising if sign == 1 else falling
-        block = buffer.at[target, span, :]
-        src = parts.at[span, pl.ds(target * width, width)] if first else block
-        return c.make(slots[chunk, target, sign], src, block, head=head + sign)
-
-    def arrived(chunk, target, sign):
-        span = pl.ds(chunk * count, count)
-        block = (rising if sign == 1 else falling).at[target, span, :]
-        c.make(slots[chunk, target, sign], block, block, head=head).wait_recv()
-
-    def own_part(chunk, target):
-        return parts[
-            chunk * count : (chunk + 1) * count, target * width : (target + 1) * width
-        ].astype(jnp.float32)
-
-    orders = {1: list(range(size - 1, 0, -1)), -1: list(range(size - 1))}
-    def begin(chunk):
-        for sign in (1, -1):
-            end = 0 if sign == 1 else size - 1
-            for target in orders[sign]:
-                pl.when(head == end)(
-                    lambda target=target, sign=sign: message(chunk, target, sign, True).start()
-                )
-                ahead = head < target if sign == 1 else head > target
-
-                def drain(target=target, sign=sign, ahead=ahead):
-                    pl.when(ahead)(lambda: message(chunk, target, sign, False).wait_send())
-
-                c.to_drain.append(drain)
-
-    def add(chunk, target, sign):
-        span = slice(chunk * count, (chunk + 1) * count)
-        arrived(chunk, target, sign)
-        buffer = rising if sign == 1 else falling
-        buffer[target, span, :] = (
-            buffer[target, span, :].astype(jnp.float32) + own_part(chunk, target)
-        ).astype(buffer.dtype)
-        message(chunk, target, sign, False).start()
-
-    def pass_on(chunk, distance):
-        for sign in (1, -1):
-            here = distance if sign == 1 else size - 1 - distance
-
-            @pl.when(head == here)
-            def passes(sign=sign, here=here):
-                for target in orders[sign]:
-                    if (target - here) * sign > 0:
-                        add(chunk, target, sign)
-
-    def finish_chunk(chunk):
-        span = slice(chunk * count, (chunk + 1) * count)
-        for target in range(size):
-
-            @pl.when(head == target)
-            def finish(target=target):
-                total = own_part(chunk, target)
-                if target > 0:
-                    arrived(chunk, target, 1)
-                    total = total + rising[target, span, :].astype(jnp.float32)
-                if target < size - 1:
-                    arrived(chunk, target, -1)
-                    total = total + falling[target, span, :].astype(jnp.float32)
-                mine[span, :] = total.astype(mine.dtype)
-
-    planes, stores, plane_sent = [], [], []
-    lag = max(size - 2, 1)
-    begin(0)
-    for turn in range(chunk_count + lag + 2):
-        if turn + 1 < chunk_count:
-            begin(turn + 1)
-        for distance in range(1, size - 1):
-            if 0 <= turn - distance + 1 < chunk_count:
-                pass_on(turn - distance + 1, distance)
-        if 0 <= turn - lag < chunk_count:
-            chunk = turn - lag
-            finish_chunk(chunk)
-            base = chunk * count
-            plane = PlaneGather(
-                c,
-                lambda low, n, base=base: mine.at[pl.ds(base + low, n), :],
-                lambda index, low, n, base=base: back_all.at[index, pl.ds(base + low, n), :],
-                count,
-            )
-            plane.first()
-            stores.append(
-                c.local(
-                    mine.at[pl.ds(base, count), :],
-                    back_all.at[place.data, pl.ds(base, count), :],
-                )
-            )
-            planes.append(plane)
-        if 0 <= turn - lag - 1 < chunk_count:
-            planes[turn - lag - 1].second()
-            planes[turn - lag - 1].third()
-        if 0 <= turn - lag - 2 < chunk_count:
-            planes[turn - lag - 2].fourth()
-        if turn == 0:
+                target = size - 1 - index if sign == 1 else index
+                ahead = target > head if sign == 1 else target < head
+                pl.when(ahead)(lambda sign=sign, target=target: visit(sign, target))
+            return carry
+
+        lax.fori_loop(0, size - 1, step, 0)
+
+    def relay(turn):
+        def visit(sign, target):
+            buffer = rising if sign == 1 else falling
+            starts = head == (0 if sign == 1 else size - 1)
+            product(target, turn)
+            for half in range(halves):
+                own = whole_part.at[span(half), :]
+
+                @pl.when(jnp.logical_not(starts))
+                def add():
+                    message(sign, target, turn, half).wait_recv()
+                    own[...] = own[...] + buffer[target, turn, span(half), :].astype(jnp.float32)
+
+                buffer[target, turn, span(half), :] = own[...].astype(buffer.dtype)
+                message(sign, target, turn, half).start()
+
+        each_target(visit)
+
+    def plane_copy(step, turn, half):
+        block = back.at[turn, place.data, span(half), :]
+        chip = lax.rem(place.chip + step, place.chips)
+        return pltpu.make_async_remote_copy(
+            src_ref=block,
+            dst_ref=block,
+            send_sem=plane_send.at[step, turn, half],
+            recv_sem=plane_recv.at[step, turn, half],
+            device_id={"dp": chip * cores + place.core, "head": head},
+            device_id_type=MESH,
+        )
+
+    def source(step):
+        return lax.rem(place.chip - step + place.chips, place.chips) * cores + place.core
+
+    def flip_copy(step, turn, half):
+        block = back.at[turn, source(step), span(half), :]
+        return pltpu.make_async_remote_copy(
+            src_ref=block,
+            dst_ref=block,
+            send_sem=flip_send.at[step, turn, half],
+            recv_sem=flip_recv.at[step, turn, half],
+            device_id={"dp": place.at(flip=True), "head": head},
+            device_id_type=MESH,
+        )
+
+    def finish(turn):
+        product(head, turn)
+        for half in range(halves):
+            own = whole_part.at[span(half), :]
+            for sign in (1, -1):
+                buffer = rising if sign == 1 else falling
+
+                @pl.when(head > 0 if sign == 1 else head < size - 1)
+                def add():
+                    message(sign, head, turn, half).wait_recv()
+                    own[...] = own[...] + buffer[head, turn, span(half), :].astype(jnp.float32)
+
+            back[turn, place.data, span(half), :] = own[...].astype(back.dtype)
+            for step in range(1, place.chips):
+                plane_copy(step, turn, half).start()
+            flip_copy(0, turn, half).start()
+
+    def forward(turn):
+        for half in range(halves):
+            for step in range(1, place.chips):
+                plane_copy(step, turn, half).wait_recv()
+                flip_copy(step, turn, half).start()
+
+    def rotate(turn):
+        for half in range(halves):
+            for step in range(place.chips):
+                flip_copy(step, turn, half).wait_recv()
+        start = pl.multiple_of(turn * piece, piece)
+        update[:, pl.ds(start, piece)] = jnp.dot(
+            held_basis[...],
+            back[turn].reshape(place.data_size * rows, piece),
+            preferred_element_type=jnp.float32,
+        ).astype(update.dtype)
+
+    for load in loads:
+        load.wait()
+
+    def turn_of(index, carry):
+        pl.when(index < turns)(lambda: relay(index))
+
+        @pl.when(index == 0)
+        def gather_scores():
             total = partial_scores[...]
             for step, copy in zip(range(1, size), line_sent):
                 copy.wait_recv()
                 total = total + score_line[step]
             score_sum[...] = total
             for step in range(1, place.data_size):
-                other = lax.rem(place.data + step, place.data_size)
-                plane_sent.append(c.send(score_sum, score_plane.at[step], other))
+                plane_score(step).start()
+
+        for lag, stage in ((1, finish), (2, forward), (3, rotate)):
+            ready = jnp.logical_and(index >= lag, index < turns + lag)
+            pl.when(ready)(lambda lag=lag, stage=stage: stage(index - lag))
+        return carry
+
+    lax.fori_loop(0, turns + 3, turn_of, 0)
     total = score_sum[...]
-    for step, copy in zip(range(1, place.data_size), plane_sent):
-        copy.wait_recv()
+    for step in range(1, place.data_size):
+        plane_score(step).wait_recv()
         total = total + score_plane[step]
     scores[...] = total
-    for plane in planes:
-        plane.last()
-    for store in stores:
-        store.wait()
+
+    def drain(turn, carry):
+        for half in range(halves):
+            each_target(lambda sign, target: message(sign, target, turn, half).wait_send())
+            for step in range(1, place.chips):
+                plane_copy(step, turn, half).wait_send()
+            for step in range(place.chips):
+                flip_copy(step, turn, half).wait_send()
+        return carry
+
+    lax.fori_loop(0, turns, drain, 0)
+    for step in range(1, place.data_size):
+        plane_score(step).wait_send()
     c.drain()
 
 
@@ -539,7 +579,6 @@
     data_size = lax.axis_size("dp")
     head_size = lax.axis_size("head")
     chips = data_size // cores
-    chunk_count = chunks_of(basis_out.shape[1] // data_size)
     basis_rows, full_in = basis_in.shape
     full_out = basis_out.shape[1]
     block = full_out // data_size
@@ -645,38 +684,44 @@
         name="fit_tile",
     )(damping, out_all, in_all)
 
-    back_parts = lax.dot_general(
-        scaled, columns, (((1,), (1,)), ((), ())), preferred_element_type=jnp.float32
-    ).astype(bf16)
     partial_scores = jnp.broadcast_to(
         jnp.sum(tile_scores, axis=(0, 2))[:, None], (seq_count, 128)
     )
-    back_all, score_sums = pl.pallas_call(
-        invert_kernel,
+    piece = min(width, most_columns)
+    turns = width // piece
+    dma = pltpu.SemaphoreType.DMA
+    update, score_sums = pl.pallas_call(
+        finish_kernel,
         out_shape=(
-            shaped(data_size, block, width),
+            shaped(block, width),
             shaped(seq_count, 128, dtype=jnp.float32),
         ),
-        in_specs=[IN_VMEM] * 2,
-        out_specs=(ANY, IN_VMEM),
+        in_specs=[IN_VMEM, ANY, ANY, IN_VMEM],
+        out_specs=(IN_VMEM, IN_VMEM),
         scratch_shapes=[
-            pltpu.VMEM((head_size, block, width), bf16),
-            pltpu.VMEM((head_size, block, width), bf16),
-            pltpu.VMEM((block, width), bf16),
+            pltpu.VMEM((full_in, width), bf16),
+            pltpu.VMEM((block, full_out), bf16),
+            pltpu.VMEM((head_size, turns, block, piece), bf16),
+            pltpu.VMEM((head_size, turns, block, piece), bf16),
+            pltpu.VMEM((turns, data_size, block, piece), bf16),
+            pltpu.VMEM((block, piece), jnp.float32),
             pltpu.VMEM((head_size, seq_count, 128), jnp.float32),
             pltpu.VMEM((data_size, seq_count, 128), jnp.float32),
             pltpu.VMEM((seq_count, 128), jnp.float32),
-        ]
-        + sems(
-            chunk_count * (8 * data_size + 2 * head_size) + data_size + head_size, chunk_count
-        ),
+            dma((2, head_size, turns, halves)),
+            dma((2, head_size, turns, halves)),
+            dma((chips, turns, halves)),
+            dma((chips, turns, halves)),
+            dma((chips, turns, halves)),
+            dma((chips, turns, halves)),
+            dma((data_size + head_size,)),
+            dma((data_size + head_size,)),
+            dma((2,)),
+        ],
         compiler_params=talking(3),
-        name="invert",
-    )(back_parts, partial_scores)
+        name="finish",
+    )(scaled, columns, basis_out, partial_scores)
     scores = score_sums[:, 0] / math.sqrt(full_in * full_out)
-    update = jnp.dot(
-        basis_out, back_all.reshape(full_out, width), preferred_element_type=jnp.float32
-    ).astype(bf16)
     return (update, corrections, scores)
 
 

time: 254 us -> 239 us (0.941)
  matrix products: 28.9 us -> 9.57 us
  Pallas kernels: 212 us -> 215 us
    dot_general x2 -> x0, matrix products: 19.4 us -> none  [the longest x1 10.2 us: per_device(): lax.dot_general(scaled, columns, (((1,), (1,)), ((), ())), preferred_elem...]
    pallas_call x1, Pallas kernels: 105 us -> 108 us  [per_device(): pl.pallas_call(finish_kernel, out_shape=(shaped(block, width), shaped(seq...]
where the time goes in v1:
time: 239 us; the launch traced here: 238 us
  Pallas kernels  215 us (90%)
  other arithmetic  9.61 us (4%)
  matrix products  9.57 us (4%)
  local copies, waits for them, and re-layouts  2.94 us (1%)
    pallas_call x1, Pallas kernels, per_device(): pl.pallas_call(finish_kernel, out_shape=(shaped(block, width), shaped(seq...  108 us
    pallas_call x1, Pallas kernels, per_device(): pl.pallas_call(gather_inputs_kernel, out_shape=(shaped(data_size, basis_r...  48.1 us
    pallas_call x1, Pallas kernels, per_device(): pl.pallas_call(gather_rotated_kernel, out_shape=(shaped(data_size, head_s...  29.6 us
    pallas_call x1, Pallas kernels, per_device(): pl.pallas_call(scatter_kernel, out_shape=shaped(chips, data_size * share,...  20.8 us
    pallas_call x1, Pallas kernels, per_device(): pl.pallas_call(functools.partial(tile_kernel, seq_here, seq_len), grid=(s...  7.58 us
    dot_general x1, matrix products, per_device(): jnp.dot(acts_full, columns, preferred_element_type=jnp.float32).astype(bf16)  6.6 us

profile of v1, /device:TPU:11, one launch (start us, length us, event | category | flops | bytes accessed | tf_op | source)
XLA Modules:
  0.0 238.1 jit_solution(1676702731303999205)
XLA Ops:
  1.3 1.8 pad_maximum_fusion.1.acts
  3.1 1.8 pad_maximum_fusion.2
  4.9 48.1 %gather_inputs.1 = (bf16[8,512,1024]{2,1,0:T(8,128)(2,1)}, bf16[192,4096]{1,0:T(8,128)(2,1)}, bf16[48,4096]{1,0:T(8,128)(2,1)}, bf16[8,48,1024]{2,1,0:T(8,128)(2,1)}, bf16[4,512,512]{2,1,0:T(8,128)(2,1)}) custom-call(bf16[192,1024]{1,0:T(8,128)(2,1)} %pad_maximum_fusion.1.acts, bf16[4,48,1024]{2,1,0:T(8,128)(2,1)} %bitcast.39, bf16[512,4096]{1,0:T(8,128)(2,1)} %basis_in.1, ...), custom_call_target="tpu_custom_call" | custom-call | tf_op jit(solution)/shard_map/gather_inputs/pallas_call | solution.py:595
  53.0 0.0 copy-start
  53.0 0.0 copy-start.1
  53.0 0.0 copy-start.2
  53.0 6.6 %convolution_convert_fusion.rotated_in = bf16[192,1024]{1,0:T(8,128)(2,1)} fusion(bf16[192,4096]{1,0:T(8,128)(2,1)} %get-tuple-element.16, bf16[4096,1024]{1,0:T(8,128)(2,1)} %bitcast.37), kind=kOutput, calls=%fused_computation.5 | convolution fusion | flops 1610809344 | bytes 10354688 | tf_op jit(solution)/shard_map/dot_general | solution.py:643
  59.6 0.0 copy-done
  59.6 0.0 copy-done.1
  59.6 0.4 fusion.19
  60.0 0.0 copy-done.2
  60.0 0.4 fusion.6
  60.4 0.4 fusion.16
  60.7 0.4 fusion.5
  61.1 0.4 fusion.13
  61.5 0.4 fusion.4
  61.9 0.4 fusion.22
  62.3 0.4 fusion.7
  62.6 1.3 pad_maximum_fusion.parts
  64.0 20.8 %scatter_rotated.1 = bf16[4,384,512]{2,1,0:T(8,128)(2,1)} custom-call(bf16[4,384,512]{2,1,0:T(8,128)(2,1)} %pad_maximum_fusion.parts), custom_call_target="tpu_custom_call" | custom-call | tf_op jit(solution)/shard_map/scatter_rotated/pallas_call | solution.py:633
  84.8 2.5 %reduce_sum.21 = bf16[384,512]{1,0:T(8,128)(2,1)} reduce(bf16[4,384,512]{2,1,0:T(8,128)(2,1)} %scatter_rotated.1, bf16[]{:T(256)} %constant.28.clone.1), dimensions={0}, to_apply=%region_0.0 | reduce | flops 589824 | bytes 1966082 | tf_op jit(solution)/shard_map/reduce_sum | solution.py:642
  87.3 29.6 %gather_rotated.1 = (bf16[8,4,48,512]{3,2,1,0:T(8,128)(2,1)}, bf16[8,192,1024]{2,1,0:T(8,128)(2,1)}) custom-call(bf16[8,48,512]{2,1,0:T(8,128)(2,1)} %bitcast.41, bf16[192,1024]{1,0:T(8,128)(2,1)} %convolution_convert_fusion.rotated_in), custom_call_target="tpu_custom_call" | custom-call | tf_op jit(solution)/shard_map/gather_rotated/pallas_call | solution.py:644
  116.9 7.6 %fit_tile.1 = (f32[512,1024]{1,0:T(8,128)}, bf16[512,1024]{1,0:T(8,128)(2,1)}, f32[4,8,256]{2,1,0:T(8,128)}) custom-call(f32[1]{0:T(128)S(6)} %copy.11.damping, bf16[8,192,512]{2,1,0:T(8,128)(2,1)} %bitcast.40, bf16[8,192,1024]{2,1,0:T(8,128)(2,1)} %get-tuple-element.19.in_all), custom_call_target="tpu_custom_call" | custom-call | tf_op jit(solution)/shard_map/fit_tile/pallas_call | solution.py:665
  124.5 0.9 reduce_sum.22
  125.4 0.7 broadcast_in_dim.2.partial_scores
  126.0 108.4 %finish.1 = (bf16[512,1024]{1,0:T(8,128)(2,1)}, f32[8,128]{1,0:T(8,128)}) custom-call(bf16[512,1024]{1,0:T(8,128)(2,1)} %get-tuple-element.20.scaled, bf16[4096,1024]{1,0:T(8,128)(2,1)} %bitcast.38, bf16[512,4096]{1,0:T(8,128)(2,1)} %basis.1, f32[8,128]{1,0:T(8,128)} %broadcast_in_dim.2.partial_scores), custom_call_target="tpu_custom_call" | custom-call | tf_op jit(solution)/shard_map/finish/pallas_call | solution.py:693
  234.5 1.3 multiply_reduce_fusion
  235.8 2.3 copy.12
Async XLA Ops:
  53.0 6.6 %copy-start = (bf16[512,4096]{1,0:T(8,128)(2,1)S(1)}, bf16[512,4096]{1,0:T(8,128)(2,1)}, u32[]{:S(2)}) copy-start(bf16[512,4096]{1,0:T(8,128)(2,1)} %basis.1) | copy-start | bytes 12582916
  53.0 6.6 %copy-start.1 = (bf16[8,48,1024]{2,1,0:T(8,128)(2,1)S(1)}, bf16[8,48,1024]{2,1,0:T(8,128)(2,1)}, u32[]{:S(2)}) copy-start(bf16[8,48,1024]{2,1,0:T(8,128)(2,1)} %get-tuple-element.14) | copy-start | bytes 2359300
  53.0 7.0 %copy-start.2 = (bf16[4,512,512]{2,1,0:T(8,128)(2,1)S(1)}, bf16[4,512,512]{2,1,0:T(8,128)(2,1)}, u32[]{:S(2)}) copy-start(bf16[4,512,512]{2,1,0:T(8,128)(2,1)} %get-tuple-element.15) | copy-start | bytes 6291460
